TPU v7x, 512 devices: a whole 4x8x8 slice. The times are simulated.
512 devices in a mesh: row: 64 (over y, x, core), col: 8 (over z).
Axes of the slice: x: 4, y: 8, z: 8, core: 2. Of those that a mesh axis runs over, the one named last changes fastest.
Arguments:
- hamiltonian: float32 [24576, 24576], P('row', 'col'), as said below
- previous: float32 [24576, 56], P('row', 'col'), may hold values from -6 to 6
- correlation_map: int32 [24576], P('row'), may hold values from 0 to 24575, each once
- lower_cut: float32 [1], replicated, may hold values from 0.5 to 1.5
- upper_bound: float32 [1], replicated, may hold values from 5.5 to 6.5
Outputs:
- basis_out: float32 [24576, 56], P('row', 'col')
- ritz_matrix: float32 [56, 56], replicated
Inputs may be any that keep to these rules, and one draw needn't show every extreme that they name: correlation_map names every index of 0 .. 24575 exactly once. hamiltonian is symmetric.
All inputs are finite; a program needn't handle non-finite values.
Results may differ from a plain program's by a relative error of at most 0.00013.
Values sent between devices are 32-bit elements; how exact they have to be, the bound alone decides.
A program may use at most 64 MiB of HBM per device.

v0:
```python
import jax
import jax.numpy as jnp
from jax import lax
from jax.sharding import PartitionSpec as P

N = 24576
DEG = 4


def body(hamiltonian, previous, correlation_map, lower_cut, upper_bound):
    column_groups = lax.axis_size("col")
    group_width = previous.shape[1]
    width = group_width * column_groups
    centre = (upper_bound[0] + lower_cut[0]) * 0.5
    half_width = (upper_bound[0] - lower_cut[0]) * 0.5
    spread = lax.all_gather(previous, "row", axis=0, tiled=True)
    start_block = jnp.take(spread, correlation_map, axis=0)

    def operate_on(vectors):
        spread_rows = lax.all_gather(vectors, "row", axis=0, tiled=True)
        wanted = lax.all_to_all(spread_rows, "col", split_axis=0, concat_axis=1, tiled=True)
        partial_sum = jnp.dot(hamiltonian, wanted, precision=lax.Precision.HIGHEST)
        return lax.psum_scatter(partial_sum, "col", scatter_dimension=1, tiled=True)

    earlier = start_block
    current = (operate_on(earlier) - centre * earlier) / half_width
    for repeat in range(DEG - 1):
        following = 2.0 * (operate_on(current) - centre * current) / half_width - earlier
        earlier = current
        current = following
    column_index = lax.axis_index("col")
    full_rows = lax.all_gather(current, "col", axis=1, tiled=True)
    empty = jnp.zeros((width, width), jnp.float32)
    block_rows = jnp.dot(current.T, full_rows, precision=lax.Precision.HIGHEST)
    gram_part = lax.dynamic_update_slice_in_dim(empty, block_rows, column_index * group_width, 0)
    gram_total = lax.psum(gram_part, ("row", "col"))
    applied = operate_on(current)
    block_cols = jnp.dot(full_rows.T, applied, precision=lax.Precision.HIGHEST)
    proj_total = lax.psum(
        lax.dynamic_update_slice_in_dim(empty, block_cols, column_index * group_width, 1),
        ("row", "col"),
    )
    gram_matrix = gram_total / N
    projected = proj_total / N
    factor = jnp.linalg.cholesky(gram_matrix)
    identity = jnp.eye(width, dtype=jnp.float32)
    inverse = lax.linalg.triangular_solve(factor, identity, left_side=True, lower=True)
    own_columns = lax.dynamic_slice_in_dim(inverse.T, column_index * group_width, group_width, 1)
    basis_out = jnp.dot(full_rows, own_columns, precision=lax.Precision.HIGHEST)
    ritz_matrix = jnp.dot(
        jnp.dot(inverse, projected, precision=lax.Precision.HIGHEST),
        inverse.T,
        precision=lax.Precision.HIGHEST,
    )
    return (basis_out, ritz_matrix)


def solution(mesh):
    return jax.shard_map(
        body,
        mesh=mesh,
        in_specs=(P("row", "col"), P("row", "col"), P("row"), P(), P()),
        out_specs=(P("row", "col"), P()),
        check_vma=False,
    )
```

profile of v0, /device:TPU:1, one launch (start us, length us, event | category | flops | bytes accessed | tf_op | source)
XLA Modules:
  0.0 1014.7 jit_solution(17210025577529272954)
XLA Ops:
  8.6 0.8 copy.41
  9.4 70.1 %all_gather.21 = f32[24576,7]{1,0:T(8,128)} all-gather(f32[384,7]{1,0:T(8,128)S(1)} %copy.41), channel_id=1, replica_groups=mesh['row'=64,'col'=8] {'row'}, dimensions={0}, use_global_device_ids=true | all-gather | bytes 698880 | tf_op jit(solution)/shard_map/all_gather | solution.py:16
  79.6 5.7 gather_fusion
  85.4 48.9 %all_gather.22 = f32[24576,7]{0,1:T(8,128)S(1)} all-gather(f32[384,7]{0,1:T(8,128)S(1)} %broadcast_select_fusion), channel_id=1, replica_groups=mesh['row'=64,'col'=8] {'row'}, dimensions={0}, use_global_device_ids=true | all-gather | bytes 698880 | tf_op jit(solution)/shard_map/all_gather | solution.py:20
  134.3 30.6 %all_to_all.95 = f32[8,3072,7]{1,2,0:T(8,128)S(1)} all-to-all(f32[8,3072,7]{1,2,0:T(8,128)S(1)} %bitcast.63), channel_id=1, replica_groups=mesh['row'=64,'col'=8] {'col'}, dimensions={0} | all-to-all | bytes 1376256 | tf_op jit(solution)/shard_map/all_to_all | solution.py:21
  164.9 7.4 convolution_bitcast_fusion.4
  173.7 1.3 dynamic-slice.4
  175.7 61.5 %all-reduce.12.cloned.1.call-done = f32[384,56]{0,1:T(8,128)} async-done(((f32[384,56]{0,1:T(8,128)}), f32[384,56]{0,1:T(8,128)}) %all-reduce.12.cloned.1.call-update) | async-done | bytes 86032
  237.9 56.2 %all_gather.23 = f32[24576,7]{0,1:T(8,128)S(1)} all-gather(f32[384,7]{0,1:T(8,128)S(1)} %fusion.18), channel_id=1, replica_groups=mesh['row'=64,'col'=8] {'row'}, dimensions={0}, use_global_device_ids=true | all-gather | bytes 698880 | tf_op jit(solution)/shard_map/all_gather | solution.py:20
  294.1 28.4 %all_to_all.96 = f32[8,3072,7]{1,2,0:T(8,128)S(1)} all-to-all(f32[8,3072,7]{1,2,0:T(8,128)S(1)} %bitcast.68), channel_id=1, replica_groups=mesh['row'=64,'col'=8] {'col'}, dimensions={0} | all-to-all | bytes 1376256 | tf_op jit(solution)/shard_map/all_to_all | solution.py:21
  322.6 7.4 convolution_bitcast_fusion.3
  330.1 64.8 %all-reduce.14.cloned.1.call-done = f32[384,56]{0,1:T(8,128)} async-done(((f32[384,56]{0,1:T(8,128)}), f32[384,56]{0,1:T(8,128)}) %all-reduce.14.cloned.1.call-update) | async-done | bytes 86032
  395.6 55.7 %all_gather.24 = f32[24576,7]{0,1:T(8,128)S(1)} all-gather(f32[384,7]{0,1:T(8,128)S(1)} %fusion.17), channel_id=1, replica_groups=mesh['row'=64,'col'=8] {'row'}, dimensions={0}, use_global_device_ids=true | all-gather | bytes 698880 | tf_op jit(solution)/shard_map/all_gather | solution.py:20
  451.4 28.6 %all_to_all.97 = f32[8,3072,7]{1,2,0:T(8,128)S(1)} all-to-all(f32[8,3072,7]{1,2,0:T(8,128)S(1)} %bitcast.69), channel_id=1, replica_groups=mesh['row'=64,'col'=8] {'col'}, dimensions={0} | all-to-all | bytes 1376256 | tf_op jit(solution)/shard_map/all_to_all | solution.py:21
  480.0 7.5 convolution_bitcast_fusion.2
  487.5 64.9 %all-reduce.16.cloned.1.call-done = f32[384,56]{0,1:T(8,128)} async-done(((f32[384,56]{0,1:T(8,128)}), f32[384,56]{0,1:T(8,128)}) %all-reduce.16.cloned.1.call-update) | async-done | bytes 86032
  552.4 0.7 fusion.14
  553.2 55.7 %all_gather.25 = f32[24576,7]{0,1:T(8,128)S(1)} all-gather(f32[384,7]{0,1:T(8,128)S(1)} %fusion.14), channel_id=1, replica_groups=mesh['row'=64,'col'=8] {'row'}, dimensions={0}, use_global_device_ids=true | all-gather | bytes 698880 | tf_op jit(solution)/shard_map/all_gather | solution.py:20
  608.8 28.4 %all_to_all.98 = f32[8,3072,7]{1,2,0:T(8,128)S(1)} all-to-all(f32[8,3072,7]{1,2,0:T(8,128)S(1)} %bitcast.70), channel_id=1, replica_groups=mesh['row'=64,'col'=8] {'col'}, dimensions={0} | all-to-all | bytes 1376256 | tf_op jit(solution)/shard_map/all_to_all | solution.py:21
  637.3 7.5 convolution_bitcast_fusion.1
  644.8 64.9 %all-reduce.18.cloned.1.call-done = f32[384,56]{0,1:T(8,128)} async-done(((f32[384,56]{0,1:T(8,128)}), f32[384,56]{0,1:T(8,128)}) %all-reduce.18.cloned.1.call-update) | async-done | bytes 86032
  710.4 60.3 %all_gather.27 = f32[24576,7]{0,1:T(8,128)} all-gather(f32[384,7]{0,1:T(8,128)S(1)} %fusion.11), channel_id=1, replica_groups=mesh['row'=64,'col'=8] {'row'}, dimensions={0}, use_global_device_ids=true | all-gather | bytes 698880 | tf_op jit(solution)/shard_map/all_gather | solution.py:20
  770.7 5.1 all-to-all-start.4
  775.8 33.0 %all-gather = f32[8,7,384]{2,1,0:T(8,128)S(1)} all-gather(f32[1,7,384]{2,1,0:T(8,128)S(1)} %bitcast.71), channel_id=1, replica_groups=mesh['row'=64,'col'=8] {'col'}, dimensions={0}, use_global_device_ids=true | all-gather | bytes 96768 | tf_op jit(solution)/shard_map/all_gather | solution.py:32
  808.9 7.4 convolution_bitcast_fusion
  816.7 74.4 %all-reduce.20.cloned.1.call-done = f32[384,56]{0,1:T(8,128)} async-done(((f32[384,56]{0,1:T(8,128)}), f32[384,56]{0,1:T(8,128)}) %all-reduce.20.cloned.1.call-update) | async-done | bytes 86032
  891.1 1.0 fusion.7
  892.4 102.7 %all-reduce.5 = (f32[56,56]{1,0:T(8,128)S(1)}, f32[56,56]{1,0:T(8,128)S(1)}) all-reduce(f32[56,56]{1,0:T(8,128)S(1)} %dynamic_update_slice.6, f32[56,56]{1,0:T(8,128)S(1)} %dynamic_update_slice.7), channel_id=1, replica_groups=mesh['row'=64,'col'=8] {'row','col'}, use_global_device_ids=true, to_apply=%region_4.5 | all-reduce | flops 6272 | bytes 50176 | tf_op jit(solution)/shard_map/psum | solution.py:36
  995.2 5.1 cholesky.16
  1001.6 4.3 custom-call.6
  1006.2 0.8 fusion.19
  1007.1 0.8 fusion.25
  (38 shorter events, 7.0 us)
Async XLA Ops:
  7.2 230.0 %all-reduce.12.cloned.1.call-start = ((), (), s32[]{:S(2)}) async-start(), calls=%async_computation.5 | async-start | bytes 172032
  172.4 222.5 %all-reduce.14.cloned.1.call-start = ((), (), s32[]{:S(2)}) async-start(), calls=%async_computation.6 | async-start | bytes 172032
  330.0 222.4 %all-reduce.16.cloned.1.call-start = ((), (), s32[]{:S(2)}) async-start(), calls=%async_computation.7 | async-start | bytes 172032
  487.5 222.2 %all-reduce.18.cloned.1.call-start = ((), (), s32[]{:S(2)}) async-start(), calls=%async_computation.8 | async-start | bytes 172032
  770.7 38.1 %all-to-all-start.4 = ((f32[8,3072,7]{1,2,0:T(8,128)}), f32[8,3072,7]{1,2,0:T(8,128)S(1)}, u32[]{:S(2)}, u32[]{:S(2)}) async-start(f32[8,3072,7]{1,2,0:T(8,128)} %bitcast.19), calls=%async_computation.4 | async-start | bytes 1572864 | tf_op jit(solution)/shard_map/all_to_all | solution.py:21
  775.8 115.3 %all-reduce.20.cloned.1.call-start = ((), (), s32[]{:S(2)}) async-start(), calls=%async_computation.9 | async-start | bytes 172032
Sparse Core Ops, SparseCore 0:
  172.5 64.5 all-reduce.11
  330.2 64.6 all-reduce.13
  487.6 64.7 all-reduce.15
  644.9 64.7 all-reduce.17
  816.5 74.5 all-reduce.19
where the time goes:
time: 1020 us; the launch traced here: 1010 us
  blocking collectives  598 us (59%)
  waiting for transfers between devices  330 us (32%)
  matrix products  40.4 us (4%)
  between operations  16.1 us (2%)
  other arithmetic  15.1 us (1%)
    unnamed x10, waiting for transfers between devices  330 us
    all_gather x5, blocking collectives, operate_on(): spread_rows = lax.all_gather(vectors, 'row', axis=0, tiled=True)  277 us
    all_to_all x4, blocking collectives, operate_on(): lax.all_to_all(spread_rows, 'col', split_axis=0, concat_axis=1, tiled=True)  116 us
    psum x1, blocking collectives, body(): gram_total = lax.psum(gram_part, ('row', 'col'))  103 us
    all_gather x1, blocking collectives, body(): spread = lax.all_gather(previous, 'row', axis=0, tiled=True)  70.1 us
    dot_general x5, matrix products, operate_on(): partial_sum = jnp.dot(hamiltonian, wanted, precision=lax.Precision.HIGHEST)  37.2 us
    all_gather x1, blocking collectives, body(): full_rows = lax.all_gather(current, 'col', axis=1, tiled=True)  33 us
  transfers between devices with their start and end apart: 6, of which 5 were waited for; matrix products, arithmetic and copies ran while one was open for 0% of the time, Pallas kernels for 0%

commit v1 on v0

v1 whole, which is shorter than its diff:
```python
import jax
import jax.numpy as jnp
from jax import lax
from jax.experimental import pallas as pl
from jax.experimental.pallas import tpu as pltpu
from jax.sharding import PartitionSpec as P

MESH = pl.DeviceIdType.MESH
F32 = jnp.float32
BF16 = jnp.bfloat16
HIGHEST = lax.Precision.HIGHEST
NSEM = 224


def far_first(n):
    return sorted(range(1, n), key=lambda d: -min(d, n - d))


def pick(k, table):
    return sum((k == i).astype(jnp.int32) * t for i, t in enumerate(table) if t)


def nt(a, b):
    return lax.dot_general(a, b, (((1,), (1,)), ((), ())), precision=HIGHEST, preferred_element_type=F32)


def kernel(
    X, Y, Z, RB, K, N,
    h_hbm, pk, idx, amod, lo, up,
    basis_ref, ritz_ref,
    hf, hcat, pall, picked, z0, xr0, lhs, acc, qb, cb, sb, xb, ysum, yb, XC, f1,
    zsum, zb, XR, f2, XT, gst, gy, gx, gc, gz, pst, pz, px, pc, py, inv_ref,
    hsem, ssem, rsem,
):
    G = K // 8
    W = K // Z
    PR = RB // 16
    r = lax.axis_index("row")
    z = lax.axis_index("col")
    core = lax.rem(r, 2)
    x = lax.rem(r // 2, X)
    y = r // (2 * X)
    other = 1 - core

    def dev(x_, y_, c_, z_):
        return ((y_ * X + x_) * 2 + c_, z_)

    zdev = lambda q: dev(x, y, core, q)
    ydev = lambda q: dev(x, q, core, z)
    xdev = lambda q: dev(q, y, core, z)
    partner = dev(x, y, other, z)
    swap = dev(x, z, core, y)

    used = [0]
    drains = []

    def alloc(n):
        base = used[0]
        used[0] += n
        assert used[0] <= NSEM
        return base

    def rc(src, dst, si, ri, to):
        return pltpu.make_async_remote_copy(
            src_ref=src, dst_ref=dst, send_sem=ssem.at[si], recv_sem=rsem.at[ri], device_id=to, device_id_type=MESH
        )

    class Axis:
        def __init__(self, n, me, devof, owners):
            self.n, self.me, self.devof, self.owners = n, me, devof, owners
            self.base = alloc(n)

        def guarded(self, who, fn):
            if self.owners >= self.n:
                fn()
            else:
                pl.when(who < self.owners)(fn)

        def ahead(self, d):
            return lax.rem(self.me + d, self.n)

        def behind(self, d):
            return lax.rem(self.me + self.n - d, self.n)

        def spread(self, at):
            def go():
                for d in far_first(self.n):
                    rc(at(self.me), at(self.me), self.base + d, self.base + self.me, self.devof(self.ahead(d))).start()

            self.guarded(self.me, go)

            def drain():
                def fin():
                    for d in far_first(self.n):
                        rc(at(self.me), at(self.me), self.base + d, self.base + self.me, self.devof(self.ahead(d))).wait_send()

                self.guarded(self.me, fin)

            drains.append(drain)

        def gathered(self, at):
            for d in reversed(far_first(self.n)):
                q = self.behind(d)

                def fin(d=d, q=q):
                    rc(at(q), at(q), self.base + d, self.base + q, self.devof(q)).wait_recv()

                self.guarded(q, fin)

        def scatter(self, src, dst):
            def each(method):
                for d in far_first(self.n):
                    p = self.ahead(d)

                    def go(d=d, p=p):
                        getattr(rc(src(p), dst(self.me), self.base + d, self.base + self.me, self.devof(p)), method)()

                    self.guarded(p, go)

            each("start")
            drains.append(lambda: each("wait_send"))

        def scattered(self, dst):
            for d in reversed(far_first(self.n)):
                q = self.behind(d)
                rc(dst(q), dst(q), self.base + d, self.base + q, self.devof(q)).wait_recv()

    hload = [pltpu.make_async_copy(h_hbm.at[:, pl.ds(i * 2 * RB, 2 * RB)], hf.at[i], hsem.at[i]) for i in range(X)]
    for c in hload:
        c.start()

    barrier = pltpu.get_barrier_semaphore()

    def greet(to):
        pl.semaphore_signal(barrier, inc=1, device_id=to, device_id_type=MESH)

    for d in range(1, Z):
        greet(zdev(lax.rem(z + d, Z)))
    for d in range(1, Y):
        greet(ydev(lax.rem(y + d, Y)))
    for d in range(1, X):
        greet(xdev(lax.rem(x + d, X)))
    greet(partner)

    @pl.when(y != z)
    def _():
        greet(swap)

    pl.semaphore_wait(barrier, (Z - 1) + (Y - 1) + (X - 1) + 1 + (y != z).astype(jnp.int32))

    centre = (up[0] + lo[0]) * 0.5
    half_width = (up[0] - lo[0]) * 0.5
    inv_hw = 1.0 / half_width

    def prow(x_, c_, y_):
        return pall.at[pl.ds(pl.multiple_of(((x_ * 2 + c_) * Y + y_) * PR, 8), PR)]

    def pblk(x_, c_):
        return pall.at[pl.ds(pl.multiple_of((x_ * 2 + c_) * Y * PR, 8), Y * PR)]

    class Plane:
        def __init__(self, blk):
            self.xa = Axis(X, x, xdev, X)
            self.cbase = alloc(X)
            self.blk = blk

        def to_partner(self, q, method):
            getattr(rc(self.blk(q, core), self.blk(q, core), self.cbase + q, self.cbase + q, partner), method)()

        def start(self):
            self.xa.spread(lambda q: self.blk(q, core))
            self.to_partner(x, "start")

        def relay(self):
            for d in reversed(far_first(X)):
                q = self.xa.behind(d)
                rc(self.blk(q, core), self.blk(q, core), self.xa.base + d, self.xa.base + q, xdev(q)).wait_recv()
                self.to_partner(q, "start")

            def drain():
                for q in range(X):
                    self.to_partner(q, "wait_send")

            drains.append(drain)

        def other_half(self, q):
            rc(self.blk(q, other), self.blk(q, other), self.cbase + q, self.cbase + q, partner).wait_recv()

    def split_h(i):
        hload[i].wait()
        diagonal = (y == z).astype(jnp.int32) * (x == i).astype(jnp.int32)
        off = core * RB - (1 - diagonal) * (8 * RB)

        hfi, hci = hf.at[i], hcat.at[i]

        @pl.loop(0, RB // 16)
        def _(t):
            row = pl.multiple_of(t * 16, 16)
            h = hfi[pl.ds(row, 16), :]
            ri = lax.broadcasted_iota(jnp.int32, h.shape, 0) + row
            ci = lax.broadcasted_iota(jnp.int32, h.shape, 1)
            h = jnp.where(ci - ri == off, h - centre, h)
            hi = h.astype(BF16)
            hci[pl.ds(row, 16), :] = hi
            hci[pl.ds(pl.multiple_of(row + RB, 16), 16), :] = (h - hi.astype(F32)).astype(BF16)

    prow(x, core, y)[...] = pk[...]
    s0y = Axis(Y, y, ydev, Y)
    s0y.spread(lambda q: prow(x, core, q))
    for i in range(X // 2):
        split_h(i)
    s0y.gathered(lambda q: prow(x, core, q))
    s0p = Plane(pblk)
    s0p.start()
    for i in range(X // 2, X):
        split_h(i)
    s0p.relay()
    for q in range(X):
        s0p.other_half(q)

    @pl.loop(0, RB // 8)
    def _(t):
        for u in range(8):
            picked[pl.ds(t * 8 + u, 1), :] = pall[pl.ds(idx[t * 8 + u], 1), :]

    lane = lax.broadcasted_iota(jnp.int32, (RB, 128), 1)
    mine = jnp.where(lane // 8 == amod[...], picked[...], 0.0)
    fold = (lax.broadcasted_iota(jnp.int32, (8, 128), 1) % 8 == lax.broadcasted_iota(jnp.int32, (8, 128), 0)).astype(F32)
    z0[z] = nt(fold, mine)
    s1 = Axis(Z, z, zdev, Z)
    s1.spread(lambda q: z0.at[q])
    s1.gathered(lambda q: z0.at[q])
    for g in range(Z):
        xr0[pl.ds(g * W, W), :] = z0[g][:W, :]

    def cat(v):
        hi = v.astype(BF16).astype(F32)
        return jnp.concatenate([hi, v - hi], axis=0).astype(BF16)

    dxs = far_first(X)

    class Wide:
        def __init__(self, i):
            self.i = i
            self.cbase = alloc(X)
            self.xa = Axis(X, x, xdev, X)
            self.ya = Axis(Y, y, ydev, G)

        def pc(self, q, method):
            i = self.i
            getattr(rc(qb.at[i, q, other], cb.at[i, q], self.cbase + q, self.cbase + q, partner), method)()

        def multiply(self, v):
            i = self.i
            c2 = cat(v)
            lhs[:, :RB] = c2
            lhs[:, RB:] = c2

            @pl.loop(0, X)
            def _(k):
                q = lax.rem(x + pick(k, dxs + [0]), X)
                p = jnp.dot(lhs[...], hcat[q], preferred_element_type=F32)
                p = p[:K] + p[K:]
                qb[i, q, 0] = p[:, :RB].reshape(G, 8, RB)
                qb[i, q, 1] = p[:, RB:].reshape(G, 8, RB)
                self.pc(q, "start")

            drains.append(lambda: [self.pc(q, "wait_send") for q in range(X)])

        def pair(self, q):
            i = self.i
            rc(cb.at[i, q], cb.at[i, q], self.cbase + q, self.cbase + q, partner).wait_recv()
            return qb[i, q, core] + cb[i, q]

        def across(self):
            i, xa = self.i, self.xa

            def cp(d):
                q = xa.ahead(d)
                return rc(sb.at[i, q], xb.at[i, x], xa.base + d, xa.base + x, xdev(q))

            for d in dxs:
                q = xa.ahead(d)
                sb[i, q] = self.pair(q)
                cp(d).start()
            drains.append(lambda: [cp(d).wait_send() for d in dxs])

        def down(self):
            i = self.i
            total = self.pair(x)
            self.xa.scattered(lambda q: xb.at[i, q])
            for d in dxs:
                total = total + xb[i, self.xa.behind(d)]
            ysum[i] = total
            self.ya.scatter(lambda q: ysum.at[i, q], lambda q: yb.at[i, q])

        def chunk(self):
            i = self.i
            yb[i, y] = ysum[i, y]
            self.ya.scattered(lambda q: yb.at[i, q])
            total = yb[i, 0]
            for q in range(1, Y):
                total = total + yb[i, q]
            return total

    class Gather:
        def __init__(self, i):
            self.i = i
            self.ya = Axis(Y, y, ydev, G)
            self.plane = Plane(lambda q, c: XC.at[i, q, c])

        def run(self):
            i = self.i
            self.ya.spread(lambda q: XC.at[i, x, core, q])
            self.ya.gathered(lambda q: XC.at[i, x, core, q])
            self.plane.start()
            self.plane.relay()

    class Tall:
        def __init__(self, i):
            self.i = i
            self.rs = Axis(Z, z, zdev, G)
            self.ag = Axis(Z, z, zdev, G)

        def multiply(self, plane):
            i = self.i
            acc[...] = jnp.zeros_like(acc)

            @pl.loop(0, X)
            def _(k):
                q = lax.rem(x + pick(k, [0] + dxs[::-1]), X)
                plane.other_half(q)
                v = jnp.concatenate([XC[i, q, 0].reshape(K, RB), XC[i, q, 1].reshape(K, RB)], axis=1)
                acc[...] += lax.dot_general(cat(v), hcat[q], (((1,), (1,)), ((), ())), preferred_element_type=F32)

            a = acc[...]
            t = a[:K] + a[K:]
            t = t[:, :RB] + t[:, RB:]
            zsum[i] = t.reshape(G, 8, RB)
            self.rs.scatter(lambda q: zsum.at[i, q], lambda q: zb.at[i, q])

        def chunk(self):
            i = self.i
            zb[i, z] = zsum[i, z]
            self.rs.scattered(lambda q: zb.at[i, q])
            total = zb[i, 0]
            for q in range(1, Z):
                total = total + zb[i, q]
            return total

        def run(self):
            i = self.i
            self.ag.spread(lambda q: XR.at[i, q])
            self.ag.gathered(lambda q: XR.at[i, q])

    w0, w1, w2 = Wide(0), Wide(1), Wide(2)
    g0, g1 = Gather(0), Gather(1)
    t0, t1 = Tall(0), Tall(1)

    w0.multiply(xr0[...])
    w0.across()
    w0.down()

    @pl.when(y < G)
    def _():
        v = w0.chunk() * inv_hw
        f1[...] = v
        XC[0, x, core, y] = v

    g0.run()
    t0.multiply(g0.plane)

    @pl.when(z < G)
    def _():
        v = 2.0 * inv_hw * t0.chunk() - xr0[pl.ds(pl.multiple_of(z * 8, 8), 8), :]
        f2[...] = v
        XR[0, z] = v

    t0.run()
    w1.multiply(XR[0].reshape(K, RB))
    w1.across()
    w1.down()

    @pl.when(y < G)
    def _():
        XC[1, x, core, y] = 2.0 * inv_hw * w1.chunk() - f1[...]

    g1.run()
    t1.multiply(g1.plane)

    @pl.when(z < G)
    def _():
        XR[1, z] = 2.0 * inv_hw * t1.chunk() - f2[...]

    t1.run()

    tb = alloc(1)

    def turn(method):
        @pl.when(y != z)
        def _():
            getattr(rc(XR.at[1], XT, tb, tb, swap), method)()

    turn("start")
    drains.append(lambda: turn("wait_send"))
    w2.multiply(XR[1].reshape(K, RB))

    gay, gax, gaz = Axis(Y, y, ydev, Y), Axis(X, x, xdev, X), Axis(Z, z, zdev, G)
    paz, pax, pay = Axis(Z, z, zdev, Z), Axis(X, x, xdev, X), Axis(Y, y, ydev, G)
    gcb, pcb = alloc(1), alloc(1)

    def widen(v):
        return jnp.concatenate([v, jnp.zeros((8, 128 - K), F32)], axis=1)

    class Guard:
        def __init__(self, cond):
            self.cond = cond

        def __call__(self, fn):
            before = len(drains)
            pl.when(self.cond)(fn)
            late = drains[before:]
            del drains[before:]

            def drain():
                def fin():
                    for f in late:
                        f()

                pl.when(self.cond)(fin)

            drains.append(drain)

    gown, pown = Guard(z < G), Guard(y < G)

    def total_of(ref, n):
        t = ref[0]
        for q in range(1, n):
            t = t + ref[q]
        return t

    def swap_cores(ref, base):
        cp = lambda: rc(ref.at[core], ref.at[core], base, base, partner)
        cp().start()
        drains.append(lambda: cp().wait_send())

    def swapped(ref, base):
        rc(ref.at[other], ref.at[other], base, base, partner).wait_recv()

    @gown
    def _():
        gy[y] = widen(nt(XR[1, z], XR[1].reshape(K, RB)))
        gay.spread(lambda q: gy.at[q])

    w2.across()

    @gown
    def _():
        gay.gathered(lambda q: gy.at[q])
        gx[x] = total_of(gy, Y)
        gax.spread(lambda q: gx.at[q])

    w2.down()

    @gown
    def _():
        gax.gathered(lambda q: gx.at[q])
        gc[core] = total_of(gx, X)
        swap_cores(gc, gcb)

    @pl.when(y != z)
    def _():
        rc(XT, XT, tb, tb, swap).wait_recv()

    @pl.when(y == z)
    def _():
        XT[...] = XR[1]

    @pown
    def _():
        pz[z] = widen(nt(w2.chunk(), XT[...].reshape(K, RB)))
        paz.spread(lambda q: pz.at[q])

    @gown
    def _():
        swapped(gc, gcb)
        gz[z] = gc[0] + gc[1]

    gaz.spread(lambda q: gz.at[q])

    @pown
    def _():
        paz.gathered(lambda q: pz.at[q])
        px[x] = total_of(pz, Z)
        pax.spread(lambda q: px.at[q])

    gaz.gathered(lambda q: gz.at[q])
    gram = gz[...].reshape(K, 128)[:, :K] * (1.0 / N)

    eye = (lax.broadcasted_iota(jnp.int32, (K, K), 0) == lax.broadcasted_iota(jnp.int32, (K, K), 1)).astype(F32)
    work = jnp.concatenate([gram, eye], axis=1)
    rows = lax.broadcasted_iota(jnp.int32, (K, 1), 0)
    scale = jnp.zeros((K, 1), F32)

    def eliminate(first, last, work, scale):
        for j in range(first, last):
            prow_ = work[j : j + 1, :]
            piv = work[j : j + 1, j : j + 1]
            col = work[:, j : j + 1]
            m = jnp.where(rows > j, col / piv, 0.0)
            scale = jnp.where(rows == j, piv, scale)
            work = work - m * prow_
        return work, scale

    work, scale = eliminate(0, K // 3, work, scale)

    @pown
    def _():
        pax.gathered(lambda q: px.at[q])
        pc[core] = total_of(px, X)
        swap_cores(pc, pcb)

    work, scale = eliminate(K // 3, K // 2, work, scale)

    @pown
    def _():
        swapped(pc, pcb)
        py[y] = pc[0] + pc[1]

    pay.spread(lambda q: py.at[q])
    work, scale = eliminate(K // 2, K, work, scale)
    inverse = work[:, K:] * lax.rsqrt(scale)
    inv_ref[...] = inverse
    own = inv_ref[pl.ds(z * W, W), :]
    basis_ref[...] = jnp.dot(own, XR[1].reshape(K, RB), precision=HIGHEST, preferred_element_type=F32)

    pay.gathered(lambda q: py.at[q])
    proj = py[...].reshape(K, 128)[:, :K] * (1.0 / N)
    proj = proj + centre * gram
    ritz_ref[...] = nt(nt(inverse, proj), inverse)

    for f in drains:
        f()


def body(hamiltonian, previous, correlation_map, lower_cut, upper_bound):
    Z = lax.axis_size("col")
    R = lax.axis_size("row")
    Y = Z
    X = R // (2 * Y)
    RB, W = previous.shape
    K = W * Z
    G = K // 8
    N = RB * R
    PR = RB // 16
    pk = jnp.pad(previous, ((0, 0), (0, 8 - W))).reshape(PR, 128)
    src = correlation_map // RB
    off = correlation_map % RB
    slot = (src % (2 * X)) * Y + src // (2 * X)
    idx = slot * PR + off // 16
    amod = (off % 16)[:, None]
    V, S = pltpu.VMEM, pltpu.SMEM
    blk = (G, 8, RB)
    scratch = [
        V((X, RB, 2 * RB), F32),
        V((X, 2 * RB, 2 * RB), BF16),
        V((R * PR, 128), F32),
        V((RB, 128), F32),
        V((Z, 8, RB), F32),
        V((K, RB), F32),
        V((2 * K, 2 * RB), BF16),
        V((2 * K, 2 * RB), F32),
        V((3, X, 2) + blk, F32),
        V((3, X) + blk, F32),
        V((3, X) + blk, F32),
        V((3, X) + blk, F32),
        V((3,) + blk, F32),
        V((3, Y, 8, RB), F32),
        V((2, X, 2) + blk, F32),
        V((8, RB), F32),
        V((2,) + blk, F32),
        V((2, Z, 8, RB), F32),
        V((2,) + blk, F32),
        V((8, RB), F32),
        V(blk, F32),
        V((8, 128), F32),
        V((Y, 8, 128), F32),
        V((X, 8, 128), F32),
        V((2, 8, 128), F32),
        V((G, 8, 128), F32),
        V((8, 128), F32),
        V((Z, 8, 128), F32),
        V((X, 8, 128), F32),
        V((2, 8, 128), F32),
        V((G, 8, 128), F32),
        V((K, K), F32),
        pltpu.SemaphoreType.DMA((X,)),
        pltpu.SemaphoreType.DMA((NSEM,)),
        pltpu.SemaphoreType.DMA((NSEM,)),
    ]
    vm = pl.BlockSpec(memory_space=V)
    sm = pl.BlockSpec(memory_space=S)
    basis_t, ritz = pl.pallas_call(
        lambda *refs: kernel(X, Y, Z, RB, K, N, *refs),
        out_shape=(jax.ShapeDtypeStruct((W, RB), F32), jax.ShapeDtypeStruct((K, K), F32)),
        in_specs=[pl.BlockSpec(memory_space=pl.ANY), vm, sm, vm, sm, sm],
        out_specs=(vm, vm),
        scratch_shapes=scratch,
        compiler_params=pltpu.CompilerParams(collective_id=0, has_side_effects=True, vmem_limit_bytes=60 * 1024 * 1024),
        name="subspace",
    )(hamiltonian, pk, idx, amod, lower_cut, upper_bound)
    return basis_t.T, ritz


def solution(mesh):
    return jax.shard_map(
        body,
        mesh=mesh,
        in_specs=(P("row", "col"), P("row", "col"), P("row"), P(), P()),
        out_specs=(P("row", "col"), P()),
        check_vma=False,
    )
```

time: 1020 us -> 145 us (0.14)
  blocking collectives: 598 us -> 0 us
  waiting for transfers between devices: 330 us -> 0 us
  Pallas kernels: 0 us -> 136 us
  matrix products: 40.4 us -> 0 us
  between operations: 16.1 us -> 1.95 us
  other arithmetic: 15.1 us -> 1.28 us
    all_gather x7 -> x0, blocking collectives: 380 us -> none  [the longest x5 277 us: operate_on(): spread_rows = lax.all_gather(vectors, 'row', axis=0, tiled=True)]
    unnamed x10 -> x0, waiting for transfers between devices: 330 us -> none
    pallas_call x0 -> x1, Pallas kernels: none -> 136 us  [body(): pl.pallas_call(lambda *refs: kernel(X, Y, Z, RB, K, N, *refs), out_shape=...]
    all_to_all x4 -> x0, blocking collectives: 116 us -> none  [operate_on(): lax.all_to_all(spread_rows, 'col', split_axis=0, concat_axis=1, tiled=True)]
    psum x1 -> x0, blocking collectives: 103 us -> none  [body(): gram_total = lax.psum(gram_part, ('row', 'col'))]
    dot_general x10 -> x0, matrix products: 40.1 us -> none  [the longest x5 37.2 us: operate_on(): partial_sum = jnp.dot(hamiltonian, wanted, precision=lax.Precision.HIGHEST)]
    another operation x5 -> x0, other arithmetic: 10.7 us -> none  [the longest x3 5.78 us: body(): factor = jnp.linalg.cholesky(gram_matrix)]
  transfers between devices with their start and end apart: 6 -> 0, of which waited for: 5 -> 0; matrix products, arithmetic and copies ran while one was open for 0% -> 0% of each run, Pallas kernels for 0% -> 0%
where the time goes in v1:
time: 145 us
  Pallas kernels  136 us (94%)
  local copies, waits for them, and re-layouts  5.03 us (3%)
  between operations  1.95 us (1%)
    pallas_call x1, Pallas kernels, body(): pl.pallas_call(lambda *refs: kernel(X, Y, Z, RB, K, N, *refs), out_shape=...  136 us
    unnamed x3, local copies, waits for them, and re-layouts  3.5 us

profile of v1, /device:TPU:1, one launch (start us, length us, event | category | flops | bytes accessed | tf_op | source)
XLA Modules:
  0.0 144.5 jit_solution(12019419209535260915)
XLA Ops:
  0.6 0.8 copy.10
  1.5 0.7 reshape.7.refs_1_
  2.2 1.3 add_select_fusion
  3.5 0.8 broadcast_in_dim.4.refs_3_
  5.6 136.3 %subspace.1 = (f32[7,384]{1,0:T(8,128)}, f32[56,56]{1,0:T(8,128)}) custom-call(f32[384,3072]{1,0:T(8,128)} %refs_0_.1, f32[24,128]{1,0:T(8,128)} %reshape.7.refs_1_, s32[384]{0:T(512)} %get-tuple-element.7.refs_2_, s32[384,1]{1,0:T(8,128)} %broadcast_in_dim.4.refs_3_, f32[1]{0:T(128)S(6)} %copy.13.refs_4_, f32[1]{0:T(128)S(6)} %copy.14.refs_5_), custom_call_target="tpu_custom_call" | custom-call | tf_op jit(solution)/shard_map/subspace/pallas_call | solution.py:603
  141.9 1.3 copy.15
  143.2 1.4 copy.16
  (1 shorter events, 0.0 us)

commit v2 on v1

--- a/solution.py
+++ b/solution.py
@@ -29,7 +29,7 @@
     h_hbm, pk, idx, amod, lo, up,
     basis_ref, ritz_ref,
     hf, hcat, pall, picked, z0, xr0, lhs, acc, qb, cb, sb, xb, ysum, yb, XC, f1,
-    zsum, zb, XR, f2, XT, gst, gy, gx, gc, gz, pst, pz, px, pc, py, inv_ref,
+    zsum, zb, XR, f2, XT, yt, gy, gx, gc, gz, pz, px, pc, py, inv_ref,
     hsem, ssem, rsem,
 ):
     G = K // 8
@@ -49,7 +49,6 @@
     ydev = lambda q: dev(x, q, core, z)
     xdev = lambda q: dev(q, y, core, z)
     partner = dev(x, y, other, z)
-    swap = dev(x, z, core, y)
 
     used = [0]
     drains = []
@@ -142,12 +141,6 @@
         greet(xdev(lax.rem(x + d, X)))
     greet(partner)
 
-    @pl.when(y != z)
-    def _():
-        greet(swap)
-
-    pl.semaphore_wait(barrier, (Z - 1) + (Y - 1) + (X - 1) + 1 + (y != z).astype(jnp.int32))
-
     centre = (up[0] + lo[0]) * 0.5
     half_width = (up[0] - lo[0]) * 0.5
     inv_hw = 1.0 / half_width
@@ -159,17 +152,38 @@
         return pall.at[pl.ds(pl.multiple_of((x_ * 2 + c_) * Y * PR, 8), Y * PR)]
 
     class Plane:
-        def __init__(self, blk):
+        def __init__(self, blk, piece, ya):
             self.xa = Axis(X, x, xdev, X)
             self.cbase = alloc(X)
-            self.blk = blk
+            self.blk, self.piece, self.ya = blk, piece, ya
 
         def to_partner(self, q, method):
             getattr(rc(self.blk(q, core), self.blk(q, core), self.cbase + q, self.cbase + q, partner), method)()
 
-        def start(self):
-            self.xa.spread(lambda q: self.blk(q, core))
-            self.to_partner(x, "start")
+        def forward(self, q):
+            at, xa = self.piece(q), self.xa
+            for d in far_first(X):
+                rc(at, at, xa.base + d, xa.base + x, xdev(xa.ahead(d))).start()
+            rc(at, at, self.cbase + x, self.cbase + x, partner).start()
+
+        def collect(self):
+            ya, xa = self.ya, self.xa
+            ya.spread(self.piece)
+            ya.guarded(y, lambda: self.forward(y))
+            for d in reversed(far_first(Y)):
+                q = ya.behind(d)
+
+                def on(d=d, q=q):
+                    rc(self.piece(q), self.piece(q), ya.base + d, ya.base + q, ydev(q)).wait_recv()
+                    self.forward(q)
+
+                ya.guarded(q, on)
+
+            def drain():
+                for d in far_first(X):
+                    rc(self.blk(x, core), self.blk(x, core), xa.base + d, xa.base + x, xdev(xa.ahead(d))).wait_send()
+
+            drains.append(drain)
 
         def relay(self):
             for d in reversed(far_first(X)):
@@ -205,13 +219,11 @@
             hci[pl.ds(pl.multiple_of(row + RB, 16), 16), :] = (h - hi.astype(F32)).astype(BF16)
 
     prow(x, core, y)[...] = pk[...]
-    s0y = Axis(Y, y, ydev, Y)
-    s0y.spread(lambda q: prow(x, core, q))
     for i in range(X // 2):
         split_h(i)
-    s0y.gathered(lambda q: prow(x, core, q))
-    s0p = Plane(pblk)
-    s0p.start()
+    pl.semaphore_wait(barrier, (Z - 1) + (Y - 1) + (X - 1) + 1)
+    s0p = Plane(pblk, lambda q: prow(x, core, q), Axis(Y, y, ydev, Y))
+    s0p.collect()
     for i in range(X // 2, X):
         split_h(i)
     s0p.relay()
@@ -307,13 +319,10 @@
         def __init__(self, i):
             self.i = i
             self.ya = Axis(Y, y, ydev, G)
-            self.plane = Plane(lambda q, c: XC.at[i, q, c])
+            self.plane = Plane(lambda q, c: XC.at[i, q, c], lambda q: XC.at[i, x, core, q], self.ya)
 
         def run(self):
-            i = self.i
-            self.ya.spread(lambda q: XC.at[i, x, core, q])
-            self.ya.gathered(lambda q: XC.at[i, x, core, q])
-            self.plane.start()
+            self.plane.collect()
             self.plane.relay()
 
     class Tall:
@@ -388,30 +397,6 @@
     g1.run()
     t1.multiply(g1.plane)
 
-    @pl.when(z < G)
-    def _():
-        XR[1, z] = 2.0 * inv_hw * t1.chunk() - f2[...]
-
-    t1.run()
-
-    tb = alloc(1)
-
-    def turn(method):
-        @pl.when(y != z)
-        def _():
-            getattr(rc(XR.at[1], XT, tb, tb, swap), method)()
-
-    turn("start")
-    drains.append(lambda: turn("wait_send"))
-    w2.multiply(XR[1].reshape(K, RB))
-
-    gay, gax, gaz = Axis(Y, y, ydev, Y), Axis(X, x, xdev, X), Axis(Z, z, zdev, G)
-    paz, pax, pay = Axis(Z, z, zdev, Z), Axis(X, x, xdev, X), Axis(Y, y, ydev, G)
-    gcb, pcb = alloc(1), alloc(1)
-
-    def widen(v):
-        return jnp.concatenate([v, jnp.zeros((8, 128 - K), F32)], axis=1)
-
     class Guard:
         def __init__(self, cond):
             self.cond = cond
@@ -432,6 +417,26 @@
             drains.append(drain)
 
     gown, pown = Guard(z < G), Guard(y < G)
+    tya, tza = Axis(Y, y, ydev, Y), Axis(Z, z, zdev, G)
+
+    @gown
+    def _():
+        v = 2.0 * inv_hw * t1.chunk() - f2[...]
+        XR[1, z] = v
+        yt[y] = v
+
+    t1.ag.spread(lambda q: XR.at[1, q])
+    gown(lambda: tya.spread(lambda q: yt.at[q]))
+    t1.ag.gathered(lambda q: XR.at[1, q])
+
+    w2.multiply(XR[1].reshape(K, RB))
+
+    gay, gax, gaz = Axis(Y, y, ydev, Y), Axis(X, x, xdev, X), Axis(Z, z, zdev, G)
+    paz, pax, pay = Axis(Z, z, zdev, Z), Axis(X, x, xdev, X), Axis(Y, y, ydev, G)
+    gcb, pcb = alloc(1), alloc(1)
+
+    def widen(v):
+        return jnp.concatenate([v, jnp.zeros((8, 128 - K), F32)], axis=1)
 
     def total_of(ref, n):
         t = ref[0]
@@ -454,8 +459,17 @@
 
     w2.across()
 
+    def turn(d):
+        p = tza.ahead(d)
+        return rc(yt.at[p], XT.at[z], tza.base + d, tza.base + z, zdev(p))
+
     @gown
     def _():
+        tya.gathered(lambda q: yt.at[q])
+        for d in far_first(Z):
+            turn(d).start()
+        drains.append(lambda: [turn(d).wait_send() for d in far_first(Z)])
+        XT[z] = yt[z]
         gay.gathered(lambda q: gy.at[q])
         gx[x] = total_of(gy, Y)
         gax.spread(lambda q: gx.at[q])
@@ -468,31 +482,18 @@
         gc[core] = total_of(gx, X)
         swap_cores(gc, gcb)
 
-    @pl.when(y != z)
-    def _():
-        rc(XT, XT, tb, tb, swap).wait_recv()
-
-    @pl.when(y == z)
-    def _():
-        XT[...] = XR[1]
+    @gown
+    def _():
+        swapped(gc, gcb)
+        gz[z] = gc[0] + gc[1]
+
+    gaz.spread(lambda q: gz.at[q])
+    tza.gathered(lambda q: XT.at[q])
 
     @pown
     def _():
         pz[z] = widen(nt(w2.chunk(), XT[...].reshape(K, RB)))
         paz.spread(lambda q: pz.at[q])
-
-    @gown
-    def _():
-        swapped(gc, gcb)
-        gz[z] = gc[0] + gc[1]
-
-    gaz.spread(lambda q: gz.at[q])
-
-    @pown
-    def _():
-        paz.gathered(lambda q: pz.at[q])
-        px[x] = total_of(pz, Z)
-        pax.spread(lambda q: px.at[q])
 
     gaz.gathered(lambda q: gz.at[q])
     gram = gz[...].reshape(K, 128)[:, :K] * (1.0 / N)
@@ -512,7 +513,15 @@
             work = work - m * prow_
         return work, scale
 
-    work, scale = eliminate(0, K // 3, work, scale)
+    work, scale = eliminate(0, K // 2, work, scale)
+
+    @pown
+    def _():
+        paz.gathered(lambda q: pz.at[q])
+        px[x] = total_of(pz, Z)
+        pax.spread(lambda q: px.at[q])
+
+    work, scale = eliminate(K // 2, 5 * K // 8, work, scale)
 
     @pown
     def _():
@@ -520,7 +529,7 @@
         pc[core] = total_of(px, X)
         swap_cores(pc, pcb)
 
-    work, scale = eliminate(K // 3, K // 2, work, scale)
+    work, scale = eliminate(5 * K // 8, 3 * K // 4, work, scale)
 
     @pown
     def _():
@@ -528,7 +537,7 @@
         py[y] = pc[0] + pc[1]
 
     pay.spread(lambda q: py.at[q])
-    work, scale = eliminate(K // 2, K, work, scale)
+    work, scale = eliminate(3 * K // 4, K, work, scale)
     inverse = work[:, K:] * lax.rsqrt(scale)
     inv_ref[...] = inverse
     own = inv_ref[pl.ds(z * W, W), :]
@@ -583,12 +592,11 @@
         V((2,) + blk, F32),
         V((8, RB), F32),
         V(blk, F32),
-        V((8, 128), F32),
+        V((Y, 8, RB), F32),
         V((Y, 8, 128), F32),
         V((X, 8, 128), F32),
         V((2, 8, 128), F32),
         V((G, 8, 128), F32),
-        V((8, 128), F32),
         V((Z, 8, 128), F32),
         V((X, 8, 128), F32),
         V((2, 8, 128), F32),

time: 145 us -> 139 us (0.959)
  Pallas kernels: 136 us -> 131 us
    pallas_call x1, Pallas kernels: 136 us -> 131 us  [body(): pl.pallas_call(lambda *refs: kernel(X, Y, Z, RB, K, N, *refs), out_shape=...]
where the time goes in v2:
time: 139 us
  Pallas kernels  131 us (94%)
  local copies, waits for them, and re-layouts  5.03 us (4%)
  between operations  1.95 us (1%)
    pallas_call x1, Pallas kernels, body(): pl.pallas_call(lambda *refs: kernel(X, Y, Z, RB, K, N, *refs), out_shape=...  131 us
    unnamed x3, local copies, waits for them, and re-layouts  3.5 us

profile of v2, /device:TPU:1, one launch (start us, length us, event | category | flops | bytes accessed | tf_op | source)
XLA Modules:
  0.0 139.1 jit_solution(12360515278959134990)
XLA Ops:
  0.6 0.8 copy.10
  1.5 0.7 reshape.7.refs_1_
  2.2 1.3 add_select_fusion
  3.5 0.8 broadcast_in_dim.4.refs_3_
  5.6 130.8 %subspace.1 = (f32[7,384]{1,0:T(8,128)}, f32[56,56]{1,0:T(8,128)}) custom-call(f32[384,3072]{1,0:T(8,128)} %refs_0_.1, f32[24,128]{1,0:T(8,128)} %reshape.7.refs_1_, s32[384]{0:T(512)} %get-tuple-element.7.refs_2_, s32[384,1]{1,0:T(8,128)} %broadcast_in_dim.4.refs_3_, f32[1]{0:T(128)S(6)} %copy.13.refs_4_, f32[1]{0:T(128)S(6)} %copy.14.refs_5_), custom_call_target="tpu_custom_call" | custom-call | tf_op jit(solution)/shard_map/subspace/pallas_call | solution.py:611
  136.4 1.3 copy.15
  137.7 1.4 copy.16
  (1 shorter events, 0.0 us)

commit v3 on v2

--- a/solution.py
+++ b/solution.py
@@ -26,10 +26,10 @@
 
 def kernel(
     X, Y, Z, RB, K, N,
-    h_hbm, pk, idx, amod, lo, up,
+    h_hbm, pk, cmap, lo, up,
     basis_ref, ritz_ref,
     hf, hcat, pall, picked, z0, xr0, lhs, acc, qb, cb, sb, xb, ysum, yb, XC, f1,
-    zsum, zb, XR, f2, XT, yt, gy, gx, gc, gz, pz, px, pc, py, inv_ref,
+    zsum, zb, XR, f2, XT, yt, gy, gx, gz, pz, px, py, inv_ref, pos,
     hsem, ssem, rsem,
 ):
     G = K // 8
@@ -49,6 +49,8 @@
     ydev = lambda q: dev(x, q, core, z)
     xdev = lambda q: dev(q, y, core, z)
     partner = dev(x, y, other, z)
+    spot = x * 2 + core
+    mdev = lambda m: dev(m // 2, y, lax.rem(m, 2), z)
 
     used = [0]
     drains = []
@@ -139,6 +141,7 @@
         greet(ydev(lax.rem(y + d, Y)))
     for d in range(1, X):
         greet(xdev(lax.rem(x + d, X)))
+        greet(dev(lax.rem(x + d, X), y, other, z))
     greet(partner)
 
     centre = (up[0] + lo[0]) * 0.5
@@ -221,24 +224,35 @@
     prow(x, core, y)[...] = pk[...]
     for i in range(X // 2):
         split_h(i)
-    pl.semaphore_wait(barrier, (Z - 1) + (Y - 1) + (X - 1) + 1)
+    pl.semaphore_wait(barrier, (Z - 1) + (Y - 1) + 2 * (X - 1) + 1)
     s0p = Plane(pblk, lambda q: prow(x, core, q), Axis(Y, y, ydev, Y))
     s0p.collect()
     for i in range(X // 2, X):
         split_h(i)
+
+    recip = -(-65536 // PR)
+
+    @pl.loop(0, RB // 8)
+    def _(t):
+        for u in range(8):
+            row = lax.shift_right_logical(cmap[t * 8 + u], 4)
+            src = lax.shift_right_logical(row * recip, 16)
+            slot = (src & (2 * X - 1)) * Y + lax.shift_right_logical(src, (2 * X).bit_length() - 1)
+            pos[t * 8 + u] = slot * PR + row - src * PR
+
     s0p.relay()
     for q in range(X):
         s0p.other_half(q)
+    group = lax.broadcasted_iota(jnp.int32, (1, 128), 1) // 8
 
     @pl.loop(0, RB // 8)
     def _(t):
         for u in range(8):
-            picked[pl.ds(t * 8 + u, 1), :] = pall[pl.ds(idx[t * 8 + u], 1), :]
-
-    lane = lax.broadcasted_iota(jnp.int32, (RB, 128), 1)
-    mine = jnp.where(lane // 8 == amod[...], picked[...], 0.0)
+            i = t * 8 + u
+            picked[pl.ds(i, 1), :] = jnp.where(group == (cmap[i] & 15), pall[pl.ds(pos[i], 1), :], 0.0)
+
     fold = (lax.broadcasted_iota(jnp.int32, (8, 128), 1) % 8 == lax.broadcasted_iota(jnp.int32, (8, 128), 0)).astype(F32)
-    z0[z] = nt(fold, mine)
+    z0[z] = nt(fold, picked[...])
     s1 = Axis(Z, z, zdev, Z)
     s1.spread(lambda q: z0.at[q])
     s1.gathered(lambda q: z0.at[q])
@@ -431,9 +445,8 @@
 
     w2.multiply(XR[1].reshape(K, RB))
 
-    gay, gax, gaz = Axis(Y, y, ydev, Y), Axis(X, x, xdev, X), Axis(Z, z, zdev, G)
-    paz, pax, pay = Axis(Z, z, zdev, Z), Axis(X, x, xdev, X), Axis(Y, y, ydev, G)
-    gcb, pcb = alloc(1), alloc(1)
+    gay, gax, gaz = Axis(Y, y, ydev, Y), Axis(2 * X, spot, mdev, 2 * X), Axis(Z, z, zdev, G)
+    paz, pax, pay = Axis(Z, z, zdev, Z), Axis(2 * X, spot, mdev, 2 * X), Axis(Y, y, ydev, G)
 
     def widen(v):
         return jnp.concatenate([v, jnp.zeros((8, 128 - K), F32)], axis=1)
@@ -443,14 +456,6 @@
         for q in range(1, n):
             t = t + ref[q]
         return t
-
-    def swap_cores(ref, base):
-        cp = lambda: rc(ref.at[core], ref.at[core], base, base, partner)
-        cp().start()
-        drains.append(lambda: cp().wait_send())
-
-    def swapped(ref, base):
-        rc(ref.at[other], ref.at[other], base, base, partner).wait_recv()
 
     @gown
     def _():
@@ -471,7 +476,7 @@
         drains.append(lambda: [turn(d).wait_send() for d in far_first(Z)])
         XT[z] = yt[z]
         gay.gathered(lambda q: gy.at[q])
-        gx[x] = total_of(gy, Y)
+        gx[spot] = total_of(gy, Y)
         gax.spread(lambda q: gx.at[q])
 
     w2.down()
@@ -479,13 +484,7 @@
     @gown
     def _():
         gax.gathered(lambda q: gx.at[q])
-        gc[core] = total_of(gx, X)
-        swap_cores(gc, gcb)
-
-    @gown
-    def _():
-        swapped(gc, gcb)
-        gz[z] = gc[0] + gc[1]
+        gz[z] = total_of(gx, 2 * X)
 
     gaz.spread(lambda q: gz.at[q])
     tza.gathered(lambda q: XT.at[q])
@@ -518,7 +517,7 @@
     @pown
     def _():
         paz.gathered(lambda q: pz.at[q])
-        px[x] = total_of(pz, Z)
+        px[spot] = total_of(pz, Z)
         pax.spread(lambda q: px.at[q])
 
     work, scale = eliminate(K // 2, 5 * K // 8, work, scale)
@@ -526,18 +525,10 @@
     @pown
     def _():
         pax.gathered(lambda q: px.at[q])
-        pc[core] = total_of(px, X)
-        swap_cores(pc, pcb)
-
-    work, scale = eliminate(5 * K // 8, 3 * K // 4, work, scale)
-
-    @pown
-    def _():
-        swapped(pc, pcb)
-        py[y] = pc[0] + pc[1]
+        py[y] = total_of(px, 2 * X)
 
     pay.spread(lambda q: py.at[q])
-    work, scale = eliminate(3 * K // 4, K, work, scale)
+    work, scale = eliminate(5 * K // 8, K, work, scale)
     inverse = work[:, K:] * lax.rsqrt(scale)
     inv_ref[...] = inverse
     own = inv_ref[pl.ds(z * W, W), :]
@@ -563,11 +554,6 @@
     N = RB * R
     PR = RB // 16
     pk = jnp.pad(previous, ((0, 0), (0, 8 - W))).reshape(PR, 128)
-    src = correlation_map // RB
-    off = correlation_map % RB
-    slot = (src % (2 * X)) * Y + src // (2 * X)
-    idx = slot * PR + off // 16
-    amod = (off % 16)[:, None]
     V, S = pltpu.VMEM, pltpu.SMEM
     blk = (G, 8, RB)
     scratch = [
@@ -594,14 +580,13 @@
         V(blk, F32),
         V((Y, 8, RB), F32),
         V((Y, 8, 128), F32),
-        V((X, 8, 128), F32),
-        V((2, 8, 128), F32),
+        V((2 * X, 8, 128), F32),
         V((G, 8, 128), F32),
         V((Z, 8, 128), F32),
-        V((X, 8, 128), F32),
-        V((2, 8, 128), F32),
+        V((2 * X, 8, 128), F32),
         V((G, 8, 128), F32),
         V((K, K), F32),
+        S((RB,), jnp.int32),
         pltpu.SemaphoreType.DMA((X,)),
         pltpu.SemaphoreType.DMA((NSEM,)),
         pltpu.SemaphoreType.DMA((NSEM,)),
@@ -611,12 +596,12 @@
     basis_t, ritz = pl.pallas_call(
         lambda *refs: kernel(X, Y, Z, RB, K, N, *refs),
         out_shape=(jax.ShapeDtypeStruct((W, RB), F32), jax.ShapeDtypeStruct((K, K), F32)),
-        in_specs=[pl.BlockSpec(memory_space=pl.ANY), vm, sm, vm, sm, sm],
+        in_specs=[pl.BlockSpec(memory_space=pl.ANY), vm, sm, sm, sm],
         out_specs=(vm, vm),
         scratch_shapes=scratch,
         compiler_params=pltpu.CompilerParams(collective_id=0, has_side_effects=True, vmem_limit_bytes=60 * 1024 * 1024),
         name="subspace",
-    )(hamiltonian, pk, idx, amod, lower_cut, upper_bound)
+    )(hamiltonian, pk, correlation_map, lower_cut, upper_bound)
     return basis_t.T, ritz
 
 

time: 139 us -> 137 us (0.986)
  no operation moved by 1% of the time
where the time goes in v3:
time: 137 us; the launch traced here: 136 us
  Pallas kernels  130 us (95%)
  local copies, waits for them, and re-layouts  4.25 us (3%)
  between operations  1.95 us (1%)
    pallas_call x1, Pallas kernels, body(): pl.pallas_call(lambda *refs: kernel(X, Y, Z, RB, K, N, *refs), out_shape=...  130 us
    unnamed x3, local copies, waits for them, and re-layouts  3.5 us

profile of v3, /device:TPU:1, one launch (start us, length us, event | category | flops | bytes accessed | tf_op | source)
XLA Modules:
  0.0 136.4 jit_solution(2488720351379401836)
XLA Ops:
  0.6 0.8 copy.9
  1.5 0.7 reshape.7.refs_1_
  3.5 130.1 %subspace.1 = (f32[7,384]{1,0:T(8,128)}, f32[56,56]{1,0:T(8,128)}) custom-call(f32[384,3072]{1,0:T(8,128)} %refs_0_.1, f32[24,128]{1,0:T(8,128)} %reshape.7.refs_1_, s32[384]{0:T(512)} %refs_2_.1, f32[1]{0:T(128)S(6)} %copy.12.refs_3_, f32[1]{0:T(128)S(6)} %copy.13.refs_4_), custom_call_target="tpu_custom_call" | custom-call | tf_op jit(solution)/shard_map/subspace/pallas_call | solution.py:596
  133.7 1.3 copy.14
  135.0 1.4 copy.15
  (1 shorter events, 0.0 us)
